TPU v7x, 32 devices: a whole 2x2x4 slice. The times are simulated.
32 devices in a mesh: dp: 2 (over x), row: 4 (over y, core), col: 4 (over z).
Axes of the slice: x: 2, y: 2, z: 4, core: 2. Of those that a mesh axis runs over, the one named last changes fastest.
Arguments:
- tokens_in: bfloat16 [16384, 1024], P(('dp', 'col'), 'row'), may hold values from -6 to 6
- cotangent: bfloat16 [16384, 1024], P(('dp', 'col'), 'row'), may hold values from -6 to 6
- doc_lengths: int32 [8, 6], P(('dp', 'row')), may hold values from 1 to 1024, 2048 in all within a row
- mixer_gain: bfloat16 [1024], P('row'), may hold values from 0.099609375 to 1.8984375
- w_query: bfloat16 [1024, 512], P('row', 'col'), may hold values from -0.1875 to 0.1875
- w_key: bfloat16 [1024, 512], P('row', 'col'), may hold values from -0.1875 to 0.1875
- w_value: bfloat16 [1024, 1024], P('row', 'col'), may hold values from -0.1875 to 0.1875
- w_outgate: bfloat16 [1024, 1024], P('row', 'col'), may hold values from -0.1875 to 0.1875
- w_rank_in: bfloat16 [1024, 16], P('row'), may hold values from -0.1875 to 0.1875
- w_rank_out: bfloat16 [16, 512], P(None, 'col'), may hold values from -1.5 to 1.5
- decay_bias: bfloat16 [512], P('col'), may hold values from -1 to 6
- head_gain: bfloat16 [256], replicated, may hold values from 0.099609375 to 1.8984375
- w_output: bfloat16 [1024, 1024], P('col', 'row'), may hold values from -0.1875 to 0.1875
- ffn_gain: bfloat16 [1024], P('row'), may hold values from 0.099609375 to 1.8984375
- w_gate: bfloat16 [1024, 2816], P('row', 'col'), may hold values from -0.1875 to 0.1875
- w_up: bfloat16 [1024, 2816], P('row', 'col'), may hold values from -0.1875 to 0.1875
- w_down: bfloat16 [2816, 1024], P('col', 'row'), may hold values from -0.109375 to 0.109375
Outputs:
- output_rows: bfloat16 [16384, 1024], P(('dp', 'col'), 'row')
- grad_tokens: float32 [16384, 1024], P(('dp', 'col'), 'row')
- grad_mixer_gain: float32 [1024], P('row')
- grad_w_query: float32 [1024, 512], P('row', 'col')
- grad_w_key: float32 [1024, 512], P('row', 'col')
- grad_w_value: float32 [1024, 1024], P('row', 'col')
- grad_w_outgate: float32 [1024, 1024], P('row', 'col')
- grad_w_rank_in: float32 [1024, 16], P('row')
- grad_w_rank_out: float32 [16, 512], P(None, 'col')
- grad_decay_bias: float32 [512], P('col')
- grad_head_gain: float32 [256], replicated
- grad_w_output: float32 [1024, 1024], P('col', 'row')
- grad_ffn_gain: float32 [1024], P('row')
- grad_w_gate: float32 [1024, 2816], P('row', 'col')
- grad_w_up: float32 [1024, 2816], P('row', 'col')
- grad_w_down: float32 [2816, 1024], P('col', 'row')
Inputs may be any that keep to these rules, and one draw needn't show every extreme that they name: `doc_lengths`: each row sums to 2048.
All inputs are finite; a program needn't handle non-finite values.
Results may differ from a plain program's by a relative error of at most 0.015.
Values may be sent and summed in bfloat16 or wider, within the bound.
No kernel may reach another device: no remote copies, remote signals or barrier semaphores. Data moves between devices by JAX's collectives and lax.ppermute only.
A program may use at most 256 MiB of HBM per device.

v0:
```python
from functools import partial
import jax
import jax.numpy as jnp
from jax import lax
from jax.sharding import PartitionSpec as P

D = 1024
DK = 512
SEQ_LEN = 2048
SPAN = 64
HK = 128
HV = 256
exact_mode = lax.Precision.HIGHEST
norm_eps = 1e-05
head_eps = 1.0
contract_rows = (((0,), (0,)), ((), ()))
contract_cols = (((1,), (1,)), ((), ()))


def product(left, right):
    return jnp.dot(left, right, preferred_element_type=jnp.float32)


def gram_of(left, right):
    return lax.dot_general(left, right, contract_rows, preferred_element_type=jnp.float32)


def times_transpose(left, weight):
    return lax.dot_general(left, weight, contract_cols, preferred_element_type=jnp.float32)


def feature_sum(vector):
    return lax.psum(vector, "row")


def col_tokens(block):
    return lax.all_gather(block, "col", axis=0, tiled=True)


def col_parts(partial_sum):
    return lax.psum_scatter(partial_sum, "col", scatter_dimension=0, tiled=True)


def data_sum(group):
    return (
        lax.psum(group[0].astype(jnp.bfloat16), "dp").astype(jnp.float32),
        lax.psum(group[1].astype(jnp.bfloat16), "dp").astype(jnp.float32),
        lax.psum(group[2].astype(jnp.bfloat16), "dp").astype(jnp.float32),
        lax.psum(group[3].astype(jnp.bfloat16), "dp").astype(jnp.float32),
        lax.psum(group[4].astype(jnp.bfloat16), "dp").astype(jnp.float32),
        lax.psum(group[5].astype(jnp.bfloat16), "dp").astype(jnp.float32),
        lax.psum(group[6].astype(jnp.bfloat16), "dp").astype(jnp.float32),
        lax.psum(group[7].astype(jnp.bfloat16), "dp").astype(jnp.float32),
    )


def segment_ids(doc_lengths, length):
    starts = jnp.cumsum(doc_lengths, axis=-1, dtype=jnp.int32) - doc_lengths
    places = jnp.arange(length, dtype=jnp.int32)
    inside = (starts[:, None, :] <= places[None, :, None]).astype(jnp.int32)
    return jnp.sum(inside, axis=-1) - 1


def span_attend(queries, key_rows, value_rows, log_decay, segments):
    batch, length, head_count, key_dim = queries.shape
    value_dim = value_rows.shape[-1]
    spans = length // SPAN
    queries = queries.reshape(batch, spans, SPAN, head_count, key_dim)
    key_rows = key_rows.reshape(batch, spans, SPAN, head_count, key_dim)
    value_rows = value_rows.reshape(batch, spans, SPAN, head_count, value_dim)
    log_decay = log_decay.reshape(batch, spans, SPAN, head_count, key_dim)
    segments = segments.reshape(batch, spans, SPAN)
    cumulative = jnp.cumsum(log_decay, axis=2)
    final_log = cumulative[:, :, -1:]
    q_scaled = queries * jnp.exp(cumulative)
    k_scaled = key_rows * jnp.exp(-cumulative)
    k_to_end = key_rows * jnp.exp(final_log - cumulative)
    places = jnp.arange(SPAN, dtype=jnp.int32)
    causal = places[:, None] >= places[None, :]
    allowed = ((segments[..., :, None] == segments[..., None, :]) & causal).astype(jnp.float32)
    scores = (
        jnp.einsum("bnihk,bnjhk->bnhij", q_scaled, k_scaled, precision=exact_mode)
        * allowed[:, :, None]
    )
    within = jnp.einsum("bnhij,bnjhv->bnihv", scores, value_rows, precision=exact_mode)
    seg_last = segments[:, :, -1]
    tail_mask = (segments == seg_last[..., None]).astype(jnp.float32)
    update = jnp.einsum(
        "bnjhk,bnjhv->bnhkv",
        k_to_end * tail_mask[..., None, None],
        value_rows,
        precision=exact_mode,
    )
    seg_prev = jnp.concatenate([jnp.full((batch, 1), -1, jnp.int32), seg_last[:, :-1]], axis=1)
    carry_on = (seg_last == seg_prev).astype(jnp.float32)
    fade_out = jnp.exp(final_log[:, :, 0])

    def advance(carried, inputs):
        fade_now, keep_now, update_now = inputs
        before = carried
        carried = carried * (fade_now * keep_now[:, None, None])[..., None] + update_now
        return (carried, before)

    start_state = jnp.zeros((batch, head_count, key_dim, value_dim), jnp.float32)
    _, states = lax.scan(
        advance,
        start_state,
        (jnp.moveaxis(fade_out, 1, 0), jnp.moveaxis(carry_on, 1, 0), jnp.moveaxis(update, 1, 0)),
    )
    states = jnp.moveaxis(states, 0, 1)
    reads_old = (segments == seg_prev[..., None]).astype(jnp.float32)
    across = jnp.einsum(
        "bnihk,bnhkv->bnihv", q_scaled * reads_old[..., None, None], states, precision=exact_mode
    )
    return (within + across).reshape(batch, length, head_count, value_dim)


def local_mixer(segments, queries, key_rows, value_rows, gate_rows, decay_pre, gain_head):
    row_count = queries.shape[0]
    head_count = queries.shape[1] // HK
    seq_count = row_count // SEQ_LEN
    log_decay = jax.nn.log_sigmoid(decay_pre) / 16.0
    attended = span_attend(
        (queries * HK ** (-0.5)).reshape(seq_count, SEQ_LEN, head_count, HK),
        key_rows.reshape(seq_count, SEQ_LEN, head_count, HK),
        value_rows.reshape(seq_count, SEQ_LEN, head_count, HV),
        log_decay.reshape(seq_count, SEQ_LEN, head_count, HK),
        segments,
    )
    attended = attended.reshape(row_count, head_count, HV)
    normed = (
        attended
        * lax.rsqrt(jnp.mean(attended * attended, axis=-1, keepdims=True) + head_eps)
        * gain_head
    )
    return normed.reshape(row_count, head_count * HV) * jax.nn.silu(gate_rows)


def per_device(
    tokens_in,
    cotangent,
    doc_lengths,
    mixer_gain,
    w_query,
    w_key,
    w_value,
    w_outgate,
    w_rank_in,
    w_rank_out,
    decay_bias,
    head_gain,
    w_output,
    ffn_gain,
    w_gate,
    w_up,
    w_down,
):
    inputs = tokens_in.astype(jnp.float32)
    inv_one = lax.rsqrt(feature_sum(jnp.sum(inputs * inputs, axis=1)) / D + norm_eps)
    normed_one = inputs * inv_one[:, None]
    gain_one = mixer_gain.astype(jnp.float32)
    first_all = col_tokens((normed_one * gain_one).astype(jnp.bfloat16))
    partials = (
        product(first_all, w_query),
        product(first_all, w_key),
        product(first_all, w_value),
        product(first_all, w_outgate),
        product(first_all, w_rank_in),
    )
    queries, key_rows, value_rows, gate_rows, rank_rows = (
        lax.psum_scatter(partials[0], "row", scatter_dimension=0, tiled=True),
        lax.psum_scatter(partials[1], "row", scatter_dimension=0, tiled=True),
        lax.psum_scatter(partials[2], "row", scatter_dimension=0, tiled=True),
        lax.psum_scatter(partials[3], "row", scatter_dimension=0, tiled=True),
        lax.psum_scatter(partials[4], "row", scatter_dimension=0, tiled=True),
    )
    rank_out = w_rank_out.astype(jnp.float32)
    decay_pre = jnp.dot(rank_rows, rank_out, precision=exact_mode) + decay_bias.astype(jnp.float32)
    segments = segment_ids(doc_lengths, SEQ_LEN)
    mixed, mixer_pull = jax.vjp(
        partial(local_mixer, segments),
        queries,
        key_rows,
        value_rows,
        gate_rows,
        decay_pre,
        head_gain.astype(jnp.float32),
    )
    heads_all = lax.all_gather(mixed.astype(jnp.bfloat16), "row", axis=0, tiled=True)
    residual = inputs + col_parts(product(heads_all, w_output))
    inv_two = lax.rsqrt(feature_sum(jnp.sum(residual * residual, axis=1)) / D + norm_eps)
    normed_two = residual * inv_two[:, None]
    gain_two = ffn_gain.astype(jnp.float32)
    second_all = col_tokens((normed_two * gain_two).astype(jnp.bfloat16))
    gate_pre, up_pre = (
        lax.psum_scatter(product(second_all, w_gate), "row", scatter_dimension=0, tiled=True),
        lax.psum_scatter(product(second_all, w_up), "row", scatter_dimension=0, tiled=True),
    )
    sigmoid_gate = jax.nn.sigmoid(gate_pre)
    silu_gate = gate_pre * sigmoid_gate
    hidden_all = lax.all_gather(
        (silu_gate * up_pre).astype(jnp.bfloat16), "row", axis=0, tiled=True
    )
    output_rows = (residual + col_parts(product(hidden_all, w_down))).astype(jnp.bfloat16)
    grad_out = cotangent.astype(jnp.float32)
    cot_all = col_tokens(cotangent)
    grad_down_w = gram_of(hidden_all, cot_all)
    hidden_grad = lax.psum_scatter(
        times_transpose(cot_all, w_down), "row", scatter_dimension=0, tiled=True
    )
    gate_grad = (
        hidden_grad * up_pre * sigmoid_gate * (1.0 + gate_pre * (1.0 - sigmoid_gate))
    ).astype(jnp.bfloat16)
    up_grad = (hidden_grad * silu_gate).astype(jnp.bfloat16)
    gate_grad_all, up_grad_all = (
        lax.all_gather(gate_grad, "row", axis=0, tiled=True),
        lax.all_gather(up_grad, "row", axis=0, tiled=True),
    )
    grad_gate_w = gram_of(second_all, gate_grad_all)
    grad_up_w = gram_of(second_all, up_grad_all)
    second_grad = col_parts(
        times_transpose(gate_grad_all, w_gate) + times_transpose(up_grad_all, w_up)
    )
    scaled_two = second_grad * gain_two
    gain_two_part = jnp.sum(second_grad * normed_two, axis=0)
    mean_two = feature_sum(jnp.sum(scaled_two * normed_two, axis=1)) / D
    resid_grad = grad_out + inv_two[:, None] * (scaled_two - normed_two * mean_two[:, None])
    resid_all = col_tokens(resid_grad.astype(jnp.bfloat16))
    grad_output_w = gram_of(heads_all, resid_all)
    mixed_grad = lax.psum_scatter(
        times_transpose(resid_all, w_output).astype(jnp.bfloat16),
        "row",
        scatter_dimension=0,
        tiled=True,
    ).astype(jnp.float32)
    query_grad, key_grad, value_grad, outgate_grad, decay_grad, head_gain_part = mixer_pull(
        mixed_grad
    )
    decay_low = decay_grad.astype(jnp.bfloat16)
    sent = (
        query_grad.astype(jnp.bfloat16),
        key_grad.astype(jnp.bfloat16),
        value_grad.astype(jnp.bfloat16),
        outgate_grad.astype(jnp.bfloat16),
        decay_low,
    )
    query_all, key_all, value_all, outgate_all, decay_all = (
        lax.all_gather(sent[0], "row", axis=0, tiled=True),
        lax.all_gather(sent[1], "row", axis=0, tiled=True),
        lax.all_gather(sent[2], "row", axis=0, tiled=True),
        lax.all_gather(sent[3], "row", axis=0, tiled=True),
        lax.all_gather(sent[4], "row", axis=0, tiled=True),
    )
    grad_query_w = gram_of(first_all, query_all)
    grad_key_w = gram_of(first_all, key_all)
    grad_value_w = gram_of(first_all, value_all)
    grad_outgate_w = gram_of(first_all, outgate_all)
    rank_grad = lax.dot_general(
        decay_all.astype(jnp.float32),
        rank_out,
        contract_cols,
        precision=exact_mode,
        preferred_element_type=jnp.float32,
    )
    rank_in_part = lax.dot_general(
        first_all.astype(jnp.float32),
        rank_grad,
        contract_rows,
        precision=exact_mode,
        preferred_element_type=jnp.float32,
    )
    decay_local = decay_low.astype(jnp.float32)
    rank_out_part = lax.dot_general(
        rank_rows,
        decay_local,
        contract_rows,
        precision=exact_mode,
        preferred_element_type=jnp.float32,
    )
    bias_part = jnp.sum(decay_local, axis=0)
    rank_back = lax.dot_general(
        rank_grad,
        w_rank_in.astype(jnp.float32),
        contract_cols,
        precision=exact_mode,
        preferred_element_type=jnp.float32,
    )
    first_grad = col_parts(
        times_transpose(query_all, w_query)
        + times_transpose(key_all, w_key)
        + times_transpose(value_all, w_value)
        + times_transpose(outgate_all, w_outgate)
        + rank_back
    )
    scaled_one = first_grad * gain_one
    gain_one_part = jnp.sum(first_grad * normed_one, axis=0)
    mean_one = feature_sum(jnp.sum(scaled_one * normed_one, axis=1)) / D
    grad_tokens = resid_grad + inv_one[:, None] * (scaled_one - normed_one * mean_one[:, None])
    every_sum = data_sum(
        (
            grad_query_w,
            grad_key_w,
            grad_value_w,
            grad_outgate_w,
            grad_output_w,
            grad_gate_w,
            grad_up_w,
            grad_down_w,
        )
    )
    (
        grad_query_w,
        grad_key_w,
        grad_value_w,
        grad_outgate_w,
        grad_output_w,
        grad_gate_w,
        grad_up_w,
        grad_down_w,
    ) = every_sum
    row_at = lax.axis_index("row")
    col_at = lax.axis_index("col")
    feature_width = mixer_gain.shape[0]
    key_width = decay_bias.shape[0]
    rank_count = w_rank_in.shape[1]
    full_one = lax.dynamic_update_slice(
        jnp.zeros((D,), jnp.float32), gain_one_part, (row_at * feature_width,)
    )
    full_two = lax.dynamic_update_slice(
        jnp.zeros((D,), jnp.float32), gain_two_part, (row_at * feature_width,)
    )
    full_rank_in = lax.dynamic_update_slice(
        jnp.zeros((D, rank_count), jnp.float32), rank_in_part, (row_at * feature_width, 0)
    )
    full_rank_out = lax.dynamic_update_slice(
        jnp.zeros((rank_count, DK), jnp.float32), rank_out_part, (0, col_at * key_width)
    )
    full_bias = lax.dynamic_update_slice(
        jnp.zeros((DK,), jnp.float32), bias_part, (col_at * key_width,)
    )
    sum_one, sum_two, sum_rank_in, sum_rank_out, sum_bias, sum_head = lax.psum(
        (full_one, full_two, full_rank_in, full_rank_out, full_bias, head_gain_part),
        ("dp", "row", "col"),
    )
    grad_mixer_gain = lax.dynamic_slice_in_dim(sum_one, row_at * feature_width, feature_width, 0)
    grad_ffn_gain = lax.dynamic_slice_in_dim(sum_two, row_at * feature_width, feature_width, 0)
    grad_rank_in = lax.dynamic_slice_in_dim(sum_rank_in, row_at * feature_width, feature_width, 0)
    grad_rank_out = lax.dynamic_slice_in_dim(sum_rank_out, col_at * key_width, key_width, 1)
    grad_bias = lax.dynamic_slice_in_dim(sum_bias, col_at * key_width, key_width, 0)
    return (
        output_rows,
        grad_tokens,
        grad_mixer_gain,
        grad_query_w,
        grad_key_w,
        grad_value_w,
        grad_outgate_w,
        grad_rank_in,
        grad_rank_out,
        grad_bias,
        sum_head,
        grad_output_w,
        grad_ffn_gain,
        grad_gate_w,
        grad_up_w,
        grad_down_w,
    )


def solution(mesh):
    in_specs = (
        P(("dp", "col"), "row"),
        P(("dp", "col"), "row"),
        P(("dp", "row"), None),
        P("row"),
        P("row", "col"),
        P("row", "col"),
        P("row", "col"),
        P("row", "col"),
        P("row", None),
        P(None, "col"),
        P("col"),
        P(),
        P("col", "row"),
        P("row"),
        P("row", "col"),
        P("row", "col"),
        P("col", "row"),
    )
    out_specs = (
        P(("dp", "col"), "row"),
        P(("dp", "col"), "row"),
        P("row"),
        P("row", "col"),
        P("row", "col"),
        P("row", "col"),
        P("row", "col"),
        P("row", None),
        P(None, "col"),
        P("col"),
        P(),
        P("col", "row"),
        P("row"),
        P("row", "col"),
        P("row", "col"),
        P("col", "row"),
    )
    return jax.shard_map(
        per_device, mesh=mesh, in_specs=in_specs, out_specs=out_specs, check_vma=False
    )
```

profile of v0, /device:TPU:0, one launch (start us, length us, event | category | flops | bytes accessed | tf_op | source)
XLA Modules:
  0.0 2682.3 jit_solution(10545545383116421357)
XLA Ops:
  8.9 8.6 psum.126
  21.3 81.1 %all-gather.14.cloned.1.call-done = bf16[8192,256]{1,0:T(8,128)(2,1)} async-done(((bf16[2048,256]{1,0:T(8,128)(2,1)}), bf16[8192,256]{1,0:T(8,128)(2,1)}) %all-gather.14.cloned.1.call-update) | async-done | bytes 4194320 | tf_op jit(solution)/shard_map/all_gather | solution.py:37
  102.4 4.2 fusion.96
  106.7 5.4 fusion.95
  113.0 5.5 fusion.97
  119.3 6.8 fusion.94
  130.0 7.4 fusion.99
  144.3 29.8 %reduce-scatter.16.cloned.1.call-done = f32[2048,128]{1,0:T(8,128)} async-done(((f32[8192,128]{1,0:T(8,128)}), f32[2048,128]{1,0:T(8,128)}) %reduce-scatter.16.cloned.1.call-update) | async-done | bytes 1048592 | tf_op jit(solution)/shard_map/reduce_scatter | solution.py:171
  175.4 45.7 %reduce-scatter.20.cloned.1.call-done = f32[2048,128]{1,0:T(8,128)} async-done(((f32[8192,128]{1,0:T(8,128)}), f32[2048,128]{1,0:T(8,128)}) %reduce-scatter.20.cloned.1.call-update) | async-done | bytes 1048592 | tf_op jit(solution)/shard_map/reduce_scatter | solution.py:172
  221.1 5.3 convolution_select_fusion.1
  226.3 68.6 %reduce-scatter.14.cloned.1.call-done = f32[2048,256]{1,0:T(8,128)} async-done(((f32[8192,256]{1,0:T(8,128)}), f32[2048,256]{1,0:T(8,128)}) %reduce-scatter.14.cloned.1.call-update) | async-done | bytes 2097168 | tf_op jit(solution)/shard_map/reduce_scatter | solution.py:173
  294.9 5.3 fusion.98
  300.2 6.8 convolution_bitcast_fusion.1
  310.3 196.0 %while.36 = (s32[]{:T(128)}, f32[1,1,128,256]{3,2,1,0:T(8,128)S(1)}, f32[32,1,1,128,256]{4,3,2,1,0:T(8,128)}, f32[32,1,1,1]{0,3,2,1:T(1,128)S(1)}, f32[32,1,1,12...) while((s32[]{:T(128)}, ...), condition=%wide.region_10.11_spmd.clone, body=%wide.region_9.10_spmd.clone.sunk | while | flops 131331 | bytes 659604 | solution.py:105
  506.8 6.4 fusion.29
  520.2 34.5 %all-gather.16.cloned.1.call-done = bf16[8192,256]{1,0:T(8,128)(2,1)} async-done(((bf16[2048,256]{1,0:T(8,128)(2,1)}), bf16[8192,256]{1,0:T(8,128)(2,1)}) %all-gather.16.cloned.1.call-update) | async-done | bytes 4194320 | tf_op jit(solution)/shard_map/all_gather | solution.py:189
  554.7 6.7 fusion.100
  562.8 143.4 %reduce-scatter.24.cloned.1.call-done = f32[2048,256]{1,0:T(8,128)} async-done(((f32[8192,256]{1,0:T(8,128)}), f32[2048,256]{1,0:T(8,128)}) %reduce-scatter.24.cloned.1.call-update) | async-done | bytes 2097168 | tf_op jit(solution)/shard_map/reduce_scatter | solution.py:41
  709.0 7.0 psum.127
  719.6 69.6 %all-gather.22.cloned.1.call-done = bf16[8192,256]{1,0:T(8,128)(2,1)} async-done(((bf16[2048,256]{1,0:T(8,128)(2,1)}), bf16[8192,256]{1,0:T(8,128)(2,1)}) %all-gather.22.cloned.1.call-update) | async-done | bytes 4194320 | tf_op jit(solution)/shard_map/all_gather | solution.py:37
  789.2 14.1 fusion.104
  803.3 66.5 %all-gather.18.cloned.1.call-done = bf16[8192,256]{1,0:T(8,128)(2,1)} async-done(((bf16[2048,256]{1,0:T(8,128)(2,1)}), bf16[8192,256]{1,0:T(8,128)(2,1)}) %all-gather.18.cloned.1.call-update) | async-done | bytes 4194320 | tf_op jit(solution)/shard_map/all_gather | solution.py:37
  869.9 16.6 fusion.101
  886.6 16.8 fusion.102
  903.5 130.5 %reduce-scatter.32.cloned.1.call-done = f32[2048,704]{0,1:T(8,128)} async-done(((f32[8192,704]{0,1:T(8,128)}), f32[2048,704]{0,1:T(8,128)}) %reduce-scatter.32.cloned.1.call-update) | async-done | bytes 5767184 | tf_op jit(solution)/shard_map/reduce_scatter | solution.py:208
  1034.0 165.5 %reduce-scatter.26.cloned.1.call-done = f32[2048,704]{0,1:T(8,128)} async-done(((f32[8192,704]{0,1:T(8,128)}), f32[2048,704]{0,1:T(8,128)}) %reduce-scatter.26.cloned.1.call-update) | async-done | bytes 5767184 | tf_op jit(solution)/shard_map/reduce_scatter | solution.py:196
  1199.5 165.6 %reduce-scatter.28.cloned.1.call-done = f32[2048,704]{0,1:T(8,128)} async-done(((f32[8192,704]{0,1:T(8,128)}), f32[2048,704]{0,1:T(8,128)}) %reduce-scatter.28.cloned.1.call-update) | async-done | bytes 5767184 | tf_op jit(solution)/shard_map/reduce_scatter | solution.py:197
  1365.1 10.7 multiply_convert_fusion
  1376.9 75.3 %all-gather.24.cloned.1.call-done = bf16[8192,704]{0,1:T(8,128)(2,1)} async-done(((bf16[2048,704]{0,1:T(8,128)(2,1)}), bf16[8192,704]{0,1:T(8,128)(2,1)}) %all-gather.24.cloned.1.call-update) | async-done | bytes 11534352 | tf_op jit(solution)/shard_map/all_gather | solution.py:216
  1452.1 12.1 fusion.105
  1464.3 65.4 %all-gather.26.cloned.1.call-done = bf16[8192,704]{0,1:T(8,128)(2,1)} async-done(((bf16[2048,704]{0,1:T(8,128)(2,1)}), bf16[8192,704]{0,1:T(8,128)(2,1)}) %all-gather.26.cloned.1.call-update) | async-done | bytes 11534352 | tf_op jit(solution)/shard_map/all_gather | solution.py:217
  1529.7 13.6 convolution_add_fusion.4
  1543.4 144.7 %reduce-scatter.34.cloned.1.call-done = f32[2048,256]{1,0:T(8,128)} async-done(((f32[8192,256]{1,0:T(8,128)}), f32[2048,256]{1,0:T(8,128)}) %reduce-scatter.34.cloned.1.call-update) | async-done | bytes 2097168 | tf_op jit(solution)/shard_map/reduce_scatter | solution.py:41
  1691.1 6.4 psum.128
  1700.6 81.2 %all-gather.28.cloned.1.call-done = bf16[8192,256]{1,0:T(8,128)(2,1)} async-done(((bf16[2048,256]{1,0:T(8,128)(2,1)}), bf16[8192,256]{1,0:T(8,128)(2,1)}) %all-gather.28.cloned.1.call-update) | async-done | bytes 4194320 | tf_op jit(solution)/shard_map/all_gather | solution.py:37
  1781.8 5.5 convolution_convert_fusion
  1788.1 42.4 %reduce-scatter.36.cloned.1.call-done = bf16[2048,256]{1,0:T(8,128)(2,1)} async-done(((bf16[8192,256]{1,0:T(8,128)(2,1)}), bf16[2048,256]{1,0:T(8,128)(2,1)}) %reduce-scatter.36.cloned.1.call-update) | async-done | bytes 1048592 | tf_op jit(solution)/shard_map/reduce_scatter | solution.py:230
  1837.0 9.4 convolution_bitcast_fusion
  1849.0 171.0 %while.37 = (s32[]{:T(128)}, f32[1,1,128,256]{3,2,1,0:T(8,128)S(1)}, f32[32,1,1,128]{3,2,1,0:T(1,128)S(1)}, f32[32,1,1,128,256]{4,3,2,1,0:T(8,128)}, f32[32,1,1,...) while((s32[]{:T(128)}, ...), condition=%wide.region_27.28_spmd.clone, body=%wide.region_25.27_spmd.clone.sunk | while | flops 196612 | bytes 1313960 | solution.py:105
  2020.0 8.2 fusion.72
  2031.5 4.4 fusion.37
  2052.4 4.2 add_convert_fusion
  2057.7 9.6 convolution_convert_fusion.1
  2067.3 6.8 convolution_convert_fusion.2
  2074.2 9.9 convolution_convert_fusion.3
  2094.9 4.9 convolution_convert_fusion.8
  2099.8 4.4 fusion.106
  2104.3 15.3 all-gather.32.cloned.1.call-done
  2119.6 4.9 convolution_convert_fusion.7
  2124.6 8.3 convolution_add_fusion.3
  2132.9 23.4 all-gather.34.cloned.1.call-done
  2156.3 5.4 convolution_convert_fusion.6
  2161.7 31.1 %all-gather.36.cloned.1.call-done = bf16[8192,256]{1,0:T(8,128)(2,1)} async-done(((bf16[2048,256]{1,0:T(8,128)(2,1)}), bf16[8192,256]{1,0:T(8,128)(2,1)}) %all-gather.36.cloned.1.call-update) | async-done | bytes 4194320 | tf_op jit(solution)/shard_map/all_gather | solution.py:251
  2192.7 5.4 convolution_convert_fusion.5
  2198.3 6.1 convolution_add_fusion.2
  2205.7 5.7 convolution_add_fusion
  2212.4 11.1 fusion.103
  2225.0 92.7 %all-reduce.6.cloned.1.call-done = f32[1024,16]{0,1:T(8,128)} async-done(((f32[1024,16]{0,1:T(8,128)}), f32[1024,16]{0,1:T(8,128)}) %all-reduce.6.cloned.1.call-update) | async-done | bytes 65552 | tf_op jit(solution)/shard_map/psum | solution.py:341
  2319.0 56.0 %all-reduce.8.cloned.1.call-done = (bf16[256,128]{1,0:T(8,128)(2,1)}, bf16[256,128]{1,0:T(8,128)(2,1)}, bf16[256,256]{1,0:T(8,128)(2,1)}, bf16[256,256]{1,0:T(8,...) async-done(((bf16[256,128]{1,0:T(8,128)(2,1)}, bf16[256,128]{1,0:T(8,128)(2,1)}, ...) | async-done | bytes 1605648 | tf_op jit(solution)/shard_map/psum | solution.py:46
  2387.0 134.9 %reduce-scatter.38.cloned.1.call-done = f32[2048,256]{1,0:T(8,128)} async-done(((f32[8192,256]{1,0:T(8,128)}), f32[2048,256]{1,0:T(8,128)}) %reduce-scatter.38.cloned.1.call-update) | async-done | bytes 2097168 | tf_op jit(solution)/shard_map/reduce_scatter | solution.py:41
  2524.6 46.0 %all-reduce.1 = (f32[1024]{0:T(1024)S(1)}, f32[16,512]{1,0:T(8,128)S(1)}, f32[512]{0:T(512)S(1)}, f32[256]{0:T(256)}, f32[1024]{0:T(1024)S(1)}) all-reduce(f32[1024]{0:T(1024)S(1)} %dynamic_update_slice.46, f32[16,512]{1,0:T(8,128)S(1)} %convolution_dynamic-update-slice_fusion.1, ...), channel_id=1, replica_groups=mesh['dp'=2,'row'=4,'col'=4] {'dp','row','col'}, use_global_device_ids=true, to_apply=%region_34.35 | all-reduce | flops 11008 | bytes 88064 | tf_op jit(solution)/shard_map/psum | solution.py:341
  2572.5 6.1 psum.129
  2579.2 91.2 %reduce-scatter.30.cloned.1.call-done = f32[2048,256]{1,0:T(8,128)} async-done(((f32[8192,256]{1,0:T(8,128)}), f32[2048,256]{1,0:T(8,128)}) %reduce-scatter.30.cloned.1.call-update) | async-done | bytes 2097168 | tf_op jit(solution)/shard_map/reduce_scatter | solution.py:41
  2670.4 4.8 fusion.22
  (705 shorter events, 473.8 us)
Async XLA Ops:
  7.2 862.7 %copy-start = (bf16[256,704]{0,1:T(8,128)(2,1)S(1)}, bf16[256,704]{0,1:T(8,128)(2,1)}, u32[]{:S(2)}) copy-start(bf16[256,704]{0,1:T(8,128)(2,1)} %param.35) | copy-start | bytes 1081348
  7.2 95.2 %copy-start.55 = (bf16[256,16]{0,1:T(8,128)(2,1)S(1)}, bf16[256,16]{0,1:T(8,128)(2,1)}, u32[]{:S(2)}) copy-start(bf16[256,16]{0,1:T(8,128)(2,1)} %param.29) | copy-start | bytes 24580
  7.2 95.2 %all-gather.14.cloned.1.call-start = ((), (), s32[]{:S(2)}) async-start(), calls=%async_computation.13 | async-start | bytes 5242880 | tf_op jit(solution)/shard_map/all_gather | solution.py:37
  21.2 85.5 %copy-start.36 = (bf16[256,128]{1,0:T(8,128)(2,1)S(1)}, bf16[256,128]{1,0:T(8,128)(2,1)}, u32[]{:S(2)}) copy-start(bf16[256,128]{1,0:T(8,128)(2,1)} %param.25) | copy-start | bytes 196612
  21.2 116.6 %reduce-scatter.18.cloned.1.call-start = ((), (), s32[]{:S(2)}) async-start(), calls=%async_computation.16 | async-start | bytes 655360 | tf_op jit(solution)/shard_map/reduce_scatter | solution.py:175
  106.6 67.4 %reduce-scatter.16.cloned.1.call-start = ((), (), s32[]{:S(2)}) async-start(), calls=%async_computation.15 | async-start | bytes 5242880 | tf_op jit(solution)/shard_map/reduce_scatter | solution.py:171
  112.2 108.9 %reduce-scatter.20.cloned.1.call-start = ((), (), s32[]{:S(2)}) async-start(), calls=%async_computation.17 | async-start | bytes 5242880 | tf_op jit(solution)/shard_map/reduce_scatter | solution.py:172
  118.5 176.5 %reduce-scatter.14.cloned.1.call-start = ((), (), s32[]{:S(2)}) async-start(), calls=%async_computation.14 | async-start | bytes 10485760 | tf_op jit(solution)/shard_map/reduce_scatter | solution.py:173
  126.2 390.4 %reduce-scatter.22.cloned.1.call-start = ((), (), s32[]{:S(2)}) async-start(), calls=%async_computation.18 | async-start | bytes 10485760 | tf_op jit(solution)/shard_map/reduce_scatter | solution.py:174
  137.5 417.2 %all-gather.16.cloned.1.call-start = ((), (), s32[]{:S(2)}) async-start(), calls=%async_computation.19 | async-start | bytes 5242880 | tf_op jit(solution)/shard_map/all_gather | solution.py:189
  175.4 124.8 %copy-start.19 = (f32[2048,128]{1,0:T(8,128)}, f32[2048,128]{1,0:T(8,128)S(1)}, u32[]{:S(2)}) copy-start(f32[2048,128]{1,0:T(8,128)S(1)} %broadcast_multiply_fusion) | copy-start | bytes 3145732
  221.1 79.2 %copy-start.4 = (f32[2048,128]{1,0:T(8,128)S(1)}, f32[2048,128]{1,0:T(8,128)}, u32[]{:S(2)}) copy-start(f32[2048,128]{1,0:T(8,128)} %reduce-scatter.20.cloned.1.call-done) | copy-start | bytes 3145732
  513.2 48.2 %copy-start.12 = (f32[32,256,64]{1,2,0:T(8,128)}, f32[32,256,64]{1,2,0:T(8,128)S(1)}, u32[]{:S(2)}) copy-start(f32[32,256,64]{1,2,0:T(8,128)S(1)} %get-tuple-element.419) | copy-start | bytes 6291460
  520.1 186.1 %reduce-scatter.24.cloned.1.call-start = ((), (), s32[]{:S(2)}) async-start(), calls=%async_computation.20 | async-start | bytes 10485760 | tf_op jit(solution)/shard_map/reduce_scatter | solution.py:41
  561.5 227.7 %all-gather.22.cloned.1.call-start = ((), (), s32[]{:S(2)}) async-start(), calls=%async_computation.26 | async-start | bytes 5242880 | tf_op jit(solution)/shard_map/all_gather | solution.py:37
  562.2 307.7 %all-gather.18.cloned.1.call-start = ((), (), s32[]{:S(2)}) async-start(), calls=%async_computation.21 | async-start | bytes 5242880 | tf_op jit(solution)/shard_map/all_gather | solution.py:37
  709.0 988.4 %copy-start.2 = (f32[2048,256]{1,0:T(8,128)}, f32[2048,256]{1,0:T(8,128)S(1)}, u32[]{:S(2)}) copy-start(f32[2048,256]{1,0:T(8,128)S(1)} %get-tuple-element.398) | copy-start | bytes 6291460
  719.3 314.6 %reduce-scatter.32.cloned.1.call-start = ((), (), s32[]{:S(2)}) async-start(), calls=%async_computation.27 | async-start | bytes 28835840 | tf_op jit(solution)/shard_map/reduce_scatter | solution.py:208
  803.3 396.2 %reduce-scatter.26.cloned.1.call-start = ((), (), s32[]{:S(2)}) async-start(), calls=%async_computation.22 | async-start | bytes 28835840 | tf_op jit(solution)/shard_map/reduce_scatter | solution.py:196
  886.5 478.6 %reduce-scatter.28.cloned.1.call-start = ((), (), s32[]{:S(2)}) async-start(), calls=%async_computation.23 | async-start | bytes 28835840 | tf_op jit(solution)/shard_map/reduce_scatter | solution.py:197
  903.4 548.7 %all-gather.24.cloned.1.call-start = ((), (), s32[]{:S(2)}) async-start(), calls=%async_computation.28 | async-start | bytes 14417920 | tf_op jit(solution)/shard_map/all_gather | solution.py:216
  1375.8 153.9 %all-gather.26.cloned.1.call-start = ((), (), s32[]{:S(2)}) async-start(), calls=%async_computation.29 | async-start | bytes 14417920 | tf_op jit(solution)/shard_map/all_gather | solution.py:217
  1376.4 311.7 %reduce-scatter.34.cloned.1.call-start = ((), (), s32[]{:S(2)}) async-start(), calls=%async_computation.30 | async-start | bytes 10485760 | tf_op jit(solution)/shard_map/reduce_scatter | solution.py:41
  1543.3 144.8 %copy-start.43 = (f32[2048]{0:T(1024)S(1)}, f32[2048]{0:T(1024)}, u32[]{:S(2)}) copy-start(f32[2048]{0:T(1024)} %copy-done.42) | copy-start | bytes 24580
  1543.4 144.8 %copy-start.57 = (f32[256]{0:T(256)S(1)}, f32[256]{0:T(256)}, u32[]{:S(2)}) copy-start(f32[256]{0:T(256)} %convert_element_type.189) | copy-start | bytes 3076
  1543.4 238.4 %all-gather.28.cloned.1.call-start = ((), (), s32[]{:S(2)}) async-start(), calls=%async_computation.31 | async-start | bytes 5242880 | tf_op jit(solution)/shard_map/all_gather | solution.py:37
  1691.1 90.7 %copy-start.30 = (bf16[256,256]{1,0:T(8,128)(2,1)S(1)}, bf16[256,256]{1,0:T(8,128)(2,1)}, u32[]{:S(2)}) copy-start(bf16[256,256]{1,0:T(8,128)(2,1)} %param.33) | copy-start | bytes 393220
  1697.5 89.7 %copy-start.51 = (f32[2048]{0:T(1024)}, f32[2048]{0:T(1024)S(1)}, u32[]{:S(2)}) copy-start(f32[2048]{0:T(1024)S(1)} %broadcast_multiply_fusion.2) | copy-start | bytes 24580
  1700.5 130.0 %reduce-scatter.36.cloned.1.call-start = ((), (), s32[]{:S(2)}) async-start(), calls=%async_computation.32 | async-start | bytes 5242880 | tf_op jit(solution)/shard_map/reduce_scatter | solution.py:230
  1787.2 43.3 %copy-start.13 = (f32[32,256,64]{1,2,0:T(8,128)S(1)}, f32[32,256,64]{1,2,0:T(8,128)}, u32[]{:S(2)}) copy-start(f32[32,256,64]{1,2,0:T(8,128)} %copy-done.12) | copy-start | bytes 6291460
  1787.2 43.3 %copy-start.48 = (f32[2048]{0:T(1024)S(1)}, f32[2048]{0:T(1024)}, u32[]{:S(2)}) copy-start(f32[2048]{0:T(1024)} %rsqrt.18) | copy-start | bytes 24580
  1787.2 43.3 %copy-start.61 = (f32[256]{0:T(256)S(1)}, f32[256]{0:T(256)}, u32[]{:S(2)}) copy-start(f32[256]{0:T(256)} %convert_element_type.187) | copy-start | bytes 3076
  1787.3 46.7 %copy-start.50 = (f32[2048]{0:T(1024)S(1)}, f32[2048]{0:T(1024)}, u32[]{:S(2)}) copy-start(f32[2048]{0:T(1024)} %add.222) | copy-start | bytes 24580
  1787.3 286.9 %all-gather.20.cloned.1.call-start = ((), (), s32[]{:S(2)}) async-start(), calls=%async_computation.24 | async-start | bytes 14417920 | tf_op jit(solution)/shard_map/all_gather | solution.py:201
  1788.0 298.0 %all-gather.38.cloned.1.call-start = ((), (), s32[]{:S(2)}) async-start(), calls=%async_computation.37 | async-start | bytes 2621440 | tf_op jit(solution)/shard_map/all_gather | solution.py:252
  2020.0 9.4 copy-start.16
  2020.0 9.4 copy-start.49
  2047.4 47.5 %all-gather.30.cloned.1.call-start = ((), (), s32[]{:S(2)}) async-start(), calls=%async_computation.33 | async-start | bytes 2621440 | tf_op jit(solution)/shard_map/all_gather | solution.py:248
  2048.2 71.5 %all-gather.32.cloned.1.call-start = ((), (), s32[]{:S(2)}) async-start(), calls=%async_computation.34 | async-start | bytes 2621440 | tf_op jit(solution)/shard_map/all_gather | solution.py:249
  2048.9 107.4 %all-gather.34.cloned.1.call-start = ((), (), s32[]{:S(2)}) async-start(), calls=%async_computation.35 | async-start | bytes 5242880 | tf_op jit(solution)/shard_map/all_gather | solution.py:250
  2056.7 136.0 %all-gather.36.cloned.1.call-start = ((), (), s32[]{:S(2)}) async-start(), calls=%async_computation.36 | async-start | bytes 5242880 | tf_op jit(solution)/shard_map/all_gather | solution.py:251
  2057.3 260.4 %all-reduce.6.cloned.1.call-start = ((), (), s32[]{:S(2)}) async-start(), calls=%async_computation.39 | async-start | bytes 131072 | tf_op jit(solution)/shard_map/psum | solution.py:341
  2057.7 9.6 copy-start.17
  2074.2 9.9 copy-start.8
  2074.2 9.9 copy-start.11
  2092.2 7.6 copy-start.37
  2092.9 282.2 %all-reduce.8.cloned.1.call-start = ((), (), s32[]{:S(2)}) async-start(), calls=%async_computation.40 | async-start | bytes 3211264 | tf_op jit(solution)/shard_map/psum | solution.py:46
  2104.3 20.3 copy-start.39
  2161.7 36.6 %copy-start.32 = (bf16[256,256]{1,0:T(8,128)(2,1)S(1)}, bf16[256,256]{1,0:T(8,128)(2,1)}, u32[]{:S(2)}) copy-start(bf16[256,256]{1,0:T(8,128)(2,1)} %param.27) | copy-start | bytes 393220
  2198.2 6.2 copy-start.34
  2198.2 323.7 %reduce-scatter.38.cloned.1.call-start = ((), (), s32[]{:S(2)}) async-start(), calls=%async_computation.38 | async-start | bytes 10485760 | tf_op jit(solution)/shard_map/reduce_scatter | solution.py:41
  2198.3 6.1 copy-start.7
  2211.5 459.0 %reduce-scatter.30.cloned.1.call-start = ((), (), s32[]{:S(2)}) async-start(), calls=%async_computation.25 | async-start | bytes 10485760 | tf_op jit(solution)/shard_map/reduce_scatter | solution.py:41
  2223.6 298.3 %copy-start.18 = (bf16[2048,256]{1,0:T(8,128)(2,1)S(1)}, bf16[2048,256]{1,0:T(8,128)(2,1)}, u32[]{:S(2)}) copy-start(bf16[2048,256]{1,0:T(8,128)(2,1)} %param.21) | copy-start | bytes 3145732
  2223.6 298.3 %copy-start.47 = (f32[2048]{0:T(1024)S(1)}, f32[2048]{0:T(1024)}, u32[]{:S(2)}) copy-start(f32[2048]{0:T(1024)} %copy-done.46) | copy-start | bytes 24580
  2223.6 298.3 %copy-start.60 = (f32[256]{0:T(256)S(1)}, f32[256]{0:T(256)}, u32[]{:S(2)}) copy-start(f32[256]{0:T(256)} %copy-done.59) | copy-start | bytes 3076
  2224.6 300.0 %copy-start.64 = (f32[256]{0:T(256)S(1)}, f32[256]{0:T(256)}, u32[]{:S(2)}) copy-start(f32[256]{0:T(256)} %get-tuple-element.344) | copy-start | bytes 3076
  2224.9 445.5 %copy-start.3 = (f32[2048,256]{1,0:T(8,128)S(1)}, f32[2048,256]{1,0:T(8,128)}, u32[]{:S(2)}) copy-start(f32[2048,256]{1,0:T(8,128)} %copy-done.2) | copy-start | bytes 6291460
  2224.9 445.5 %copy-start.44 = (f32[2048]{0:T(1024)S(1)}, f32[2048]{0:T(1024)}, u32[]{:S(2)}) copy-start(f32[2048]{0:T(1024)} %copy-done.42) | copy-start | bytes 24580
  2225.0 445.5 %copy-start.52 = (f32[2048]{0:T(1024)S(1)}, f32[2048]{0:T(1024)}, u32[]{:S(2)}) copy-start(f32[2048]{0:T(1024)} %copy-done.51) | copy-start | bytes 24580
  2225.0 445.5 %copy-start.58 = (f32[256]{0:T(256)S(1)}, f32[256]{0:T(256)}, u32[]{:S(2)}) copy-start(f32[256]{0:T(256)} %convert_element_type.189) | copy-start | bytes 3076
  2375.0 10.6 copy-start.54
  2375.0 11.3 copy-start.53
  2579.2 96.0 %copy-start.1 = (bf16[256,704]{0,1:T(8,128)(2,1)S(1)}, bf16[256,704]{0,1:T(8,128)(2,1)}, u32[]{:S(2)}) copy-start(bf16[256,704]{0,1:T(8,128)(2,1)} %param.35) | copy-start | bytes 1081348
  (38 other events, 85.2 us)
Sparse Core Ops, SparseCore 0:
  21.4 81.0 all-gather.13
  106.8 20.1 reduce-scatter.17
  129.4 44.5 reduce-scatter.15
  176.5 44.5 reduce-scatter.19
  223.5 71.3 reduce-scatter.13
  297.4 71.3 reduce-scatter.21
  520.2 34.4 all-gather.15
  561.6 144.6 reduce-scatter.23
  707.8 81.3 all-gather.21
  790.6 79.2 all-gather.17
  872.5 161.4 reduce-scatter.31
  1036.4 162.9 reduce-scatter.25
  1202.1 162.9 reduce-scatter.27
  1376.0 76.1 all-gather.23
  1453.5 76.1 all-gather.25
  1543.5 144.6 reduce-scatter.33
  1700.6 81.0 all-gather.27
  1787.4 43.0 reduce-scatter.35
  1832.0 76.1 all-gather.19
  2047.5 22.5 all-gather.37
  2072.3 22.5 all-gather.29
  2097.0 22.5 all-gather.31
  2121.8 34.4 all-gather.33
  2158.3 34.4 all-gather.35
  2198.3 119.3 all-reduce.5
  2321.4 53.5 all-reduce.7
  2377.2 144.6 reduce-scatter.37
  2524.2 146.1 reduce-scatter.29
where the time goes:
time: 2690 us; the launch traced here: 2680 us
  waiting for transfers between devices  1860 us (69%)
  other arithmetic  296 us (11%)
  matrix products  274 us (10%)
  local copies, waits for them, and re-layouts  158 us (6%)
  blocking collectives  74 us (3%)
    reduce_scatter x4, waiting for transfers between devices, col_parts(): return lax.psum_scatter(partial_sum, 'col', scatter_dimension=0, tiled=True)  514 us
    all_gather x4, waiting for transfers between devices, col_tokens(): return lax.all_gather(block, 'col', axis=0, tiled=True)  298 us
    reduce_scatter x1, waiting for transfers between devices, per_device(): lax.psum_scatter(product(second_all, w_up), 'row', scatter_dimension=0, t...  166 us
    reduce_scatter x1, waiting for transfers between devices, per_device(): lax.psum_scatter(product(second_all, w_gate), 'row', scatter_dimension=0,...  165 us
    reduce_scatter x1, waiting for transfers between devices, per_device(): lax.psum_scatter(times_transpose(cot_all, w_down), 'row', scatter_dimensi...  130 us
    dynamic_update_slice x128, other arithmetic, span_attend(): lax.scan(advance, start_state, (jnp.moveaxis(fade_out, 1, 0), jnp.moveaxi...  121 us
    psum x1, waiting for transfers between devices, per_device(): lax.psum((full_one, full_two, full_rank_in, full_rank_out, full_bias, hea...  92.7 us
    dynamic_slice x128, local copies, waits for them, and re-layouts, span_attend(): lax.scan(advance, start_state, (jnp.moveaxis(fade_out, 1, 0), jnp.moveaxi...  91 us
  transfers between devices with their start and end apart: 28, of which 24 were waited for; matrix products, arithmetic and copies ran while one was open for 25% of the time, Pallas kernels for 0%

commit v1 on v0

--- a/solution.py
+++ b/solution.py
@@ -43,7 +43,7 @@
 
 def data_sum(group):
     return (
-        lax.psum(group[0].astype(jnp.bfloat16), "dp").astype(jnp.float32),
+        jnp.sum(lax.all_gather(group[0].astype(jnp.bfloat16), "dp"), axis=0).astype(jnp.float32),
         lax.psum(group[1].astype(jnp.bfloat16), "dp").astype(jnp.float32),
         lax.psum(group[2].astype(jnp.bfloat16), "dp").astype(jnp.float32),
         lax.psum(group[3].astype(jnp.bfloat16), "dp").astype(jnp.float32),

time: 2690 us -> 2690 us (level)
  transfers between devices with their start and end apart: 28 -> 28, of which waited for: 24 -> 24; matrix products, arithmetic and copies ran while one was open for 25% -> 24% of each run, Pallas kernels for 0% -> 0%
where the time goes in v1:
time: 2690 us; the launch traced here: 2680 us
  waiting for transfers between devices  1860 us (69%)
  other arithmetic  296 us (11%)
  matrix products  267 us (10%)
  local copies, waits for them, and re-layouts  159 us (6%)
  blocking collectives  79.2 us (3%)
    reduce_scatter x4, waiting for transfers between devices, col_parts(): return lax.psum_scatter(partial_sum, 'col', scatter_dimension=0, tiled=True)  515 us
    all_gather x4, waiting for transfers between devices, col_tokens(): return lax.all_gather(block, 'col', axis=0, tiled=True)  298 us
    reduce_scatter x1, waiting for transfers between devices, per_device(): lax.psum_scatter(product(second_all, w_up), 'row', scatter_dimension=0, t...  166 us
    reduce_scatter x1, waiting for transfers between devices, per_device(): lax.psum_scatter(product(second_all, w_gate), 'row', scatter_dimension=0,...  165 us
    reduce_scatter x1, waiting for transfers between devices, per_device(): lax.psum_scatter(times_transpose(cot_all, w_down), 'row', scatter_dimensi...  130 us
    dynamic_update_slice x128, other arithmetic, span_attend(): lax.scan(advance, start_state, (jnp.moveaxis(fade_out, 1, 0), jnp.moveaxi...  121 us
    dynamic_slice x128, local copies, waits for them, and re-layouts, span_attend(): lax.scan(advance, start_state, (jnp.moveaxis(fade_out, 1, 0), jnp.moveaxi...  91 us
    psum x1, waiting for transfers between devices, per_device(): lax.psum((full_one, full_two, full_rank_in, full_rank_out, full_bias, hea...  82.9 us
  transfers between devices with their start and end apart: 28, of which 24 were waited for; matrix products, arithmetic and copies ran while one was open for 24% of the time, Pallas kernels for 0%

profile of v1, /device:TPU:0, one launch (start us, length us, event | category | flops | bytes accessed | tf_op | source)
XLA Modules:
  0.0 2680.9 jit_solution(12215957015285519546)
XLA Ops:
  8.9 8.6 psum.119
  21.3 81.1 %all-gather.15.cloned.1.call-done = bf16[8192,256]{1,0:T(8,128)(2,1)} async-done(((bf16[2048,256]{1,0:T(8,128)(2,1)}), bf16[8192,256]{1,0:T(8,128)(2,1)}) %all-gather.15.cloned.1.call-update) | async-done | bytes 4194320 | tf_op jit(solution)/shard_map/all_gather | solution.py:37
  102.4 4.2 fusion.96
  106.7 5.4 fusion.95
  113.0 5.5 fusion.97
  119.3 6.8 fusion.94
  130.0 7.4 fusion.99
  144.3 29.7 %reduce-scatter.16.cloned.1.call-done = f32[2048,128]{1,0:T(8,128)} async-done(((f32[8192,128]{1,0:T(8,128)}), f32[2048,128]{1,0:T(8,128)}) %reduce-scatter.16.cloned.1.call-update) | async-done | bytes 1048592 | tf_op jit(solution)/shard_map/reduce_scatter | solution.py:171
  175.4 45.7 %reduce-scatter.20.cloned.1.call-done = f32[2048,128]{1,0:T(8,128)} async-done(((f32[8192,128]{1,0:T(8,128)}), f32[2048,128]{1,0:T(8,128)}) %reduce-scatter.20.cloned.1.call-update) | async-done | bytes 1048592 | tf_op jit(solution)/shard_map/reduce_scatter | solution.py:172
  221.0 5.3 convolution_select_fusion.1
  226.3 68.6 %reduce-scatter.14.cloned.1.call-done = f32[2048,256]{1,0:T(8,128)} async-done(((f32[8192,256]{1,0:T(8,128)}), f32[2048,256]{1,0:T(8,128)}) %reduce-scatter.14.cloned.1.call-update) | async-done | bytes 2097168 | tf_op jit(solution)/shard_map/reduce_scatter | solution.py:173
  294.9 5.3 fusion.98
  300.2 6.9 convolution_bitcast_fusion.1
  310.3 195.9 %while.36 = (s32[]{:T(128)}, f32[1,1,128,256]{3,2,1,0:T(8,128)S(1)}, f32[32,1,1,128,256]{4,3,2,1,0:T(8,128)}, f32[32,1,1,1]{0,3,2,1:T(1,128)S(1)}, f32[32,1,1,12...) while((s32[]{:T(128)}, ...), condition=%wide.region_10.11_spmd.clone, body=%wide.region_9.10_spmd.clone.sunk | while | flops 131331 | bytes 659604 | solution.py:105
  506.7 6.4 fusion.29
  520.1 34.5 %all-gather.17.cloned.1.call-done = bf16[8192,256]{1,0:T(8,128)(2,1)} async-done(((bf16[2048,256]{1,0:T(8,128)(2,1)}), bf16[8192,256]{1,0:T(8,128)(2,1)}) %all-gather.17.cloned.1.call-update) | async-done | bytes 4194320 | tf_op jit(solution)/shard_map/all_gather | solution.py:189
  554.6 6.8 fusion.100
  562.8 143.4 %reduce-scatter.24.cloned.1.call-done = f32[2048,256]{1,0:T(8,128)} async-done(((f32[8192,256]{1,0:T(8,128)}), f32[2048,256]{1,0:T(8,128)}) %reduce-scatter.24.cloned.1.call-update) | async-done | bytes 2097168 | tf_op jit(solution)/shard_map/reduce_scatter | solution.py:41
  709.0 7.0 psum.120
  719.5 69.6 %all-gather.23.cloned.1.call-done = bf16[8192,256]{1,0:T(8,128)(2,1)} async-done(((bf16[2048,256]{1,0:T(8,128)(2,1)}), bf16[8192,256]{1,0:T(8,128)(2,1)}) %all-gather.23.cloned.1.call-update) | async-done | bytes 4194320 | tf_op jit(solution)/shard_map/all_gather | solution.py:37
  789.1 14.1 fusion.104
  803.3 66.5 %all-gather.19.cloned.1.call-done = bf16[8192,256]{1,0:T(8,128)(2,1)} async-done(((bf16[2048,256]{1,0:T(8,128)(2,1)}), bf16[8192,256]{1,0:T(8,128)(2,1)}) %all-gather.19.cloned.1.call-update) | async-done | bytes 4194320 | tf_op jit(solution)/shard_map/all_gather | solution.py:37
  869.8 16.6 fusion.101
  886.5 16.9 fusion.102
  903.4 130.5 %reduce-scatter.32.cloned.1.call-done = f32[2048,704]{0,1:T(8,128)} async-done(((f32[8192,704]{0,1:T(8,128)}), f32[2048,704]{0,1:T(8,128)}) %reduce-scatter.32.cloned.1.call-update) | async-done | bytes 5767184 | tf_op jit(solution)/shard_map/reduce_scatter | solution.py:208
  1033.9 165.5 %reduce-scatter.26.cloned.1.call-done = f32[2048,704]{0,1:T(8,128)} async-done(((f32[8192,704]{0,1:T(8,128)}), f32[2048,704]{0,1:T(8,128)}) %reduce-scatter.26.cloned.1.call-update) | async-done | bytes 5767184 | tf_op jit(solution)/shard_map/reduce_scatter | solution.py:196
  1199.4 165.6 %reduce-scatter.28.cloned.1.call-done = f32[2048,704]{0,1:T(8,128)} async-done(((f32[8192,704]{0,1:T(8,128)}), f32[2048,704]{0,1:T(8,128)}) %reduce-scatter.28.cloned.1.call-update) | async-done | bytes 5767184 | tf_op jit(solution)/shard_map/reduce_scatter | solution.py:197
  1365.0 10.7 multiply_convert_fusion
  1376.8 75.3 %all-gather.25.cloned.1.call-done = bf16[8192,704]{0,1:T(8,128)(2,1)} async-done(((bf16[2048,704]{0,1:T(8,128)(2,1)}), bf16[8192,704]{0,1:T(8,128)(2,1)}) %all-gather.25.cloned.1.call-update) | async-done | bytes 11534352 | tf_op jit(solution)/shard_map/all_gather | solution.py:216
  1452.1 12.1 fusion.105
  1464.2 65.4 %all-gather.27.cloned.1.call-done = bf16[8192,704]{0,1:T(8,128)(2,1)} async-done(((bf16[2048,704]{0,1:T(8,128)(2,1)}), bf16[8192,704]{0,1:T(8,128)(2,1)}) %all-gather.27.cloned.1.call-update) | async-done | bytes 11534352 | tf_op jit(solution)/shard_map/all_gather | solution.py:217
  1529.6 13.6 convolution_add_fusion.4
  1543.4 144.7 %reduce-scatter.34.cloned.1.call-done = f32[2048,256]{1,0:T(8,128)} async-done(((f32[8192,256]{1,0:T(8,128)}), f32[2048,256]{1,0:T(8,128)}) %reduce-scatter.34.cloned.1.call-update) | async-done | bytes 2097168 | tf_op jit(solution)/shard_map/reduce_scatter | solution.py:41
  1691.0 6.4 psum.121
  1700.5 81.2 %all-gather.29.cloned.1.call-done = bf16[8192,256]{1,0:T(8,128)(2,1)} async-done(((bf16[2048,256]{1,0:T(8,128)(2,1)}), bf16[8192,256]{1,0:T(8,128)(2,1)}) %all-gather.29.cloned.1.call-update) | async-done | bytes 4194320 | tf_op jit(solution)/shard_map/all_gather | solution.py:37
  1781.7 5.4 convolution_convert_fusion
  1788.0 42.4 %reduce-scatter.36.cloned.1.call-done = bf16[2048,256]{1,0:T(8,128)(2,1)} async-done(((bf16[8192,256]{1,0:T(8,128)(2,1)}), bf16[2048,256]{1,0:T(8,128)(2,1)}) %reduce-scatter.36.cloned.1.call-update) | async-done | bytes 1048592 | tf_op jit(solution)/shard_map/reduce_scatter | solution.py:230
  1836.9 9.4 convolution_bitcast_fusion
  1849.0 171.0 %while.37 = (s32[]{:T(128)}, f32[1,1,128,256]{3,2,1,0:T(8,128)S(1)}, f32[32,1,1,128]{3,2,1,0:T(1,128)S(1)}, f32[32,1,1,128,256]{4,3,2,1,0:T(8,128)}, f32[32,1,1,...) while((s32[]{:T(128)}, ...), condition=%wide.region_27.28_spmd.clone, body=%wide.region_25.27_spmd.clone.sunk | while | flops 196612 | bytes 1313960 | solution.py:105
  2020.0 8.2 fusion.72
  2031.4 4.4 fusion.37
  2039.4 4.1 fusion.54
  2052.4 4.2 add_convert_fusion
  2057.7 9.6 convolution_convert_fusion.1
  2067.3 6.8 convolution_convert_fusion.2
  2074.1 9.9 convolution_convert_fusion.3
  2094.9 4.8 convolution_convert_fusion.7
  2099.7 19.9 all-gather.31.cloned.1.call-done
  2122.5 4.5 convolution_add_fusion.3
  2127.0 29.3 %all-gather.35.cloned.1.call-done = bf16[8192,256]{1,0:T(8,128)(2,1)} async-done(((bf16[2048,256]{1,0:T(8,128)(2,1)}), bf16[8192,256]{1,0:T(8,128)(2,1)}) %all-gather.35.cloned.1.call-update) | async-done | bytes 4194320 | tf_op jit(solution)/shard_map/all_gather | solution.py:250
  2156.2 5.4 convolution_convert_fusion.6
  2161.7 31.1 %all-gather.37.cloned.1.call-done = bf16[8192,256]{1,0:T(8,128)(2,1)} async-done(((bf16[2048,256]{1,0:T(8,128)(2,1)}), bf16[8192,256]{1,0:T(8,128)(2,1)}) %all-gather.37.cloned.1.call-update) | async-done | bytes 4194320 | tf_op jit(solution)/shard_map/all_gather | solution.py:251
  2192.7 5.4 convolution_convert_fusion.5
  2198.3 6.1 convolution_add_fusion.2
  2205.7 5.7 convolution_add_fusion
  2212.4 11.1 fusion.103
  2228.9 5.2 all-gather
  2234.9 82.9 %all-reduce.6.cloned.1.call-done = f32[1024,16]{0,1:T(8,128)} async-done(((f32[1024,16]{0,1:T(8,128)}), f32[1024,16]{0,1:T(8,128)}) %all-reduce.6.cloned.1.call-update) | async-done | bytes 65552 | tf_op jit(solution)/shard_map/psum | solution.py:341
  2319.0 54.6 %all-reduce.8.cloned.1.call-done = (bf16[256,128]{1,0:T(8,128)(2,1)}, bf16[256,256]{1,0:T(8,128)(2,1)}, bf16[256,256]{1,0:T(8,128)(2,1)}, bf16[256,256]{1,0:T(8,...) async-done(((bf16[256,128]{1,0:T(8,128)(2,1)}, bf16[256,256]{1,0:T(8,128)(2,1)}, bf16[256,256]{1,0:T(8,128)(2,1)}, ...) | async-done | bytes 1540112 | tf_op jit(solution)/shard_map/psum | solution.py:47
  2384.9 135.5 %reduce-scatter.38.cloned.1.call-done = f32[2048,256]{1,0:T(8,128)} async-done(((f32[8192,256]{1,0:T(8,128)}), f32[2048,256]{1,0:T(8,128)}) %reduce-scatter.38.cloned.1.call-update) | async-done | bytes 2097168 | tf_op jit(solution)/shard_map/reduce_scatter | solution.py:41
  2523.2 46.0 %all-reduce.1 = (f32[1024]{0:T(1024)S(1)}, f32[16,512]{1,0:T(8,128)S(1)}, f32[512]{0:T(512)S(1)}, f32[256]{0:T(256)}, f32[1024]{0:T(1024)S(1)}) all-reduce(f32[1024]{0:T(1024)S(1)} %dynamic_update_slice.46, f32[16,512]{1,0:T(8,128)S(1)} %convolution_dynamic-update-slice_fusion.1, ...), channel_id=1, replica_groups=mesh['dp'=2,'row'=4,'col'=4] {'dp','row','col'}, use_global_device_ids=true, to_apply=%region_34.35 | all-reduce | flops 11008 | bytes 88064 | tf_op jit(solution)/shard_map/psum | solution.py:341
  2571.0 6.1 psum.122
  2577.8 91.2 %reduce-scatter.30.cloned.1.call-done = f32[2048,256]{1,0:T(8,128)} async-done(((f32[8192,256]{1,0:T(8,128)}), f32[2048,256]{1,0:T(8,128)}) %reduce-scatter.30.cloned.1.call-update) | async-done | bytes 2097168 | tf_op jit(solution)/shard_map/reduce_scatter | solution.py:41
  2669.0 4.8 fusion.22
  (709 shorter events, 476.4 us)
Async XLA Ops:
  7.2 862.6 %copy-start = (bf16[256,704]{0,1:T(8,128)(2,1)S(1)}, bf16[256,704]{0,1:T(8,128)(2,1)}, u32[]{:S(2)}) copy-start(bf16[256,704]{0,1:T(8,128)(2,1)} %param.35) | copy-start | bytes 1081348
  7.2 95.2 %copy-start.53 = (bf16[256,16]{0,1:T(8,128)(2,1)S(1)}, bf16[256,16]{0,1:T(8,128)(2,1)}, u32[]{:S(2)}) copy-start(bf16[256,16]{0,1:T(8,128)(2,1)} %param.29) | copy-start | bytes 24580
  7.2 95.2 %all-gather.15.cloned.1.call-start = ((), (), s32[]{:S(2)}) async-start(), calls=%async_computation.13 | async-start | bytes 5242880 | tf_op jit(solution)/shard_map/all_gather | solution.py:37
  21.2 85.5 %copy-start.36 = (bf16[256,128]{1,0:T(8,128)(2,1)S(1)}, bf16[256,128]{1,0:T(8,128)(2,1)}, u32[]{:S(2)}) copy-start(bf16[256,128]{1,0:T(8,128)(2,1)} %param.25) | copy-start | bytes 196612
  21.2 116.6 %reduce-scatter.18.cloned.1.call-start = ((), (), s32[]{:S(2)}) async-start(), calls=%async_computation.16 | async-start | bytes 655360 | tf_op jit(solution)/shard_map/reduce_scatter | solution.py:175
  106.6 67.4 %reduce-scatter.16.cloned.1.call-start = ((), (), s32[]{:S(2)}) async-start(), calls=%async_computation.15 | async-start | bytes 5242880 | tf_op jit(solution)/shard_map/reduce_scatter | solution.py:171
  112.1 108.9 %reduce-scatter.20.cloned.1.call-start = ((), (), s32[]{:S(2)}) async-start(), calls=%async_computation.17 | async-start | bytes 5242880 | tf_op jit(solution)/shard_map/reduce_scatter | solution.py:172
  118.4 176.4 %reduce-scatter.14.cloned.1.call-start = ((), (), s32[]{:S(2)}) async-start(), calls=%async_computation.14 | async-start | bytes 10485760 | tf_op jit(solution)/shard_map/reduce_scatter | solution.py:173
  126.2 390.4 %reduce-scatter.22.cloned.1.call-start = ((), (), s32[]{:S(2)}) async-start(), calls=%async_computation.18 | async-start | bytes 10485760 | tf_op jit(solution)/shard_map/reduce_scatter | solution.py:174
  137.5 417.1 %all-gather.17.cloned.1.call-start = ((), (), s32[]{:S(2)}) async-start(), calls=%async_computation.19 | async-start | bytes 5242880 | tf_op jit(solution)/shard_map/all_gather | solution.py:189
  175.4 124.8 %copy-start.19 = (f32[2048,128]{1,0:T(8,128)}, f32[2048,128]{1,0:T(8,128)S(1)}, u32[]{:S(2)}) copy-start(f32[2048,128]{1,0:T(8,128)S(1)} %broadcast_multiply_fusion) | copy-start | bytes 3145732
  221.0 79.2 %copy-start.4 = (f32[2048,128]{1,0:T(8,128)S(1)}, f32[2048,128]{1,0:T(8,128)}, u32[]{:S(2)}) copy-start(f32[2048,128]{1,0:T(8,128)} %reduce-scatter.20.cloned.1.call-done) | copy-start | bytes 3145732
  513.2 48.2 %copy-start.12 = (f32[32,256,64]{1,2,0:T(8,128)}, f32[32,256,64]{1,2,0:T(8,128)S(1)}, u32[]{:S(2)}) copy-start(f32[32,256,64]{1,2,0:T(8,128)S(1)} %get-tuple-element.418) | copy-start | bytes 6291460
  520.0 186.1 %reduce-scatter.24.cloned.1.call-start = ((), (), s32[]{:S(2)}) async-start(), calls=%async_computation.20 | async-start | bytes 10485760 | tf_op jit(solution)/shard_map/reduce_scatter | solution.py:41
  561.4 227.7 %all-gather.23.cloned.1.call-start = ((), (), s32[]{:S(2)}) async-start(), calls=%async_computation.26 | async-start | bytes 5242880 | tf_op jit(solution)/shard_map/all_gather | solution.py:37
  562.1 307.7 %all-gather.19.cloned.1.call-start = ((), (), s32[]{:S(2)}) async-start(), calls=%async_computation.21 | async-start | bytes 5242880 | tf_op jit(solution)/shard_map/all_gather | solution.py:37
  709.0 988.4 %copy-start.2 = (f32[2048,256]{1,0:T(8,128)}, f32[2048,256]{1,0:T(8,128)S(1)}, u32[]{:S(2)}) copy-start(f32[2048,256]{1,0:T(8,128)S(1)} %get-tuple-element.397) | copy-start | bytes 6291460
  719.3 314.6 %reduce-scatter.32.cloned.1.call-start = ((), (), s32[]{:S(2)}) async-start(), calls=%async_computation.27 | async-start | bytes 28835840 | tf_op jit(solution)/shard_map/reduce_scatter | solution.py:208
  803.2 396.2 %reduce-scatter.26.cloned.1.call-start = ((), (), s32[]{:S(2)}) async-start(), calls=%async_computation.22 | async-start | bytes 28835840 | tf_op jit(solution)/shard_map/reduce_scatter | solution.py:196
  886.4 478.6 %reduce-scatter.28.cloned.1.call-start = ((), (), s32[]{:S(2)}) async-start(), calls=%async_computation.23 | async-start | bytes 28835840 | tf_op jit(solution)/shard_map/reduce_scatter | solution.py:197
  903.4 548.7 %all-gather.25.cloned.1.call-start = ((), (), s32[]{:S(2)}) async-start(), calls=%async_computation.28 | async-start | bytes 14417920 | tf_op jit(solution)/shard_map/all_gather | solution.py:216
  1375.8 153.9 %all-gather.27.cloned.1.call-start = ((), (), s32[]{:S(2)}) async-start(), calls=%async_computation.29 | async-start | bytes 14417920 | tf_op jit(solution)/shard_map/all_gather | solution.py:217
  1376.4 311.7 %reduce-scatter.34.cloned.1.call-start = ((), (), s32[]{:S(2)}) async-start(), calls=%async_computation.30 | async-start | bytes 10485760 | tf_op jit(solution)/shard_map/reduce_scatter | solution.py:41
  1543.3 144.8 %copy-start.43 = (f32[2048]{0:T(1024)S(1)}, f32[2048]{0:T(1024)}, u32[]{:S(2)}) copy-start(f32[2048]{0:T(1024)} %copy-done.42) | copy-start | bytes 24580
  1543.3 144.8 %copy-start.57 = (f32[256]{0:T(256)S(1)}, f32[256]{0:T(256)}, u32[]{:S(2)}) copy-start(f32[256]{0:T(256)} %convert_element_type.191) | copy-start | bytes 3076
  1543.3 238.4 %all-gather.29.cloned.1.call-start = ((), (), s32[]{:S(2)}) async-start(), calls=%async_computation.31 | async-start | bytes 5242880 | tf_op jit(solution)/shard_map/all_gather | solution.py:37
  1691.0 90.7 %copy-start.30 = (bf16[256,256]{1,0:T(8,128)(2,1)S(1)}, bf16[256,256]{1,0:T(8,128)(2,1)}, u32[]{:S(2)}) copy-start(bf16[256,256]{1,0:T(8,128)(2,1)} %param.33) | copy-start | bytes 393220
  1697.4 89.8 %copy-start.51 = (f32[2048]{0:T(1024)}, f32[2048]{0:T(1024)S(1)}, u32[]{:S(2)}) copy-start(f32[2048]{0:T(1024)S(1)} %broadcast_multiply_fusion.2) | copy-start | bytes 24580
  1700.4 130.0 %reduce-scatter.36.cloned.1.call-start = ((), (), s32[]{:S(2)}) async-start(), calls=%async_computation.32 | async-start | bytes 5242880 | tf_op jit(solution)/shard_map/reduce_scatter | solution.py:230
  1787.2 43.3 %copy-start.13 = (f32[32,256,64]{1,2,0:T(8,128)S(1)}, f32[32,256,64]{1,2,0:T(8,128)}, u32[]{:S(2)}) copy-start(f32[32,256,64]{1,2,0:T(8,128)} %copy-done.12) | copy-start | bytes 6291460
  1787.2 43.3 %copy-start.48 = (f32[2048]{0:T(1024)S(1)}, f32[2048]{0:T(1024)}, u32[]{:S(2)}) copy-start(f32[2048]{0:T(1024)} %rsqrt.18) | copy-start | bytes 24580
  1787.2 43.3 %copy-start.60 = (f32[256]{0:T(256)S(1)}, f32[256]{0:T(256)}, u32[]{:S(2)}) copy-start(f32[256]{0:T(256)} %convert_element_type.189) | copy-start | bytes 3076
  1787.2 46.8 %copy-start.50 = (f32[2048]{0:T(1024)S(1)}, f32[2048]{0:T(1024)}, u32[]{:S(2)}) copy-start(f32[2048]{0:T(1024)} %add.220) | copy-start | bytes 24580
  1787.2 286.9 %all-gather.21.cloned.1.call-start = ((), (), s32[]{:S(2)}) async-start(), calls=%async_computation.24 | async-start | bytes 14417920 | tf_op jit(solution)/shard_map/all_gather | solution.py:201
  1788.0 298.0 %all-gather.39.cloned.1.call-start = ((), (), s32[]{:S(2)}) async-start(), calls=%async_computation.37 | async-start | bytes 2621440 | tf_op jit(solution)/shard_map/all_gather | solution.py:252
  2020.0 9.3 copy-start.16
  2020.0 9.3 copy-start.49
  2047.4 47.5 %all-gather.33.cloned.1.call-start = ((), (), s32[]{:S(2)}) async-start(), calls=%async_computation.34 | async-start | bytes 2621440 | tf_op jit(solution)/shard_map/all_gather | solution.py:249
  2048.1 71.5 %all-gather.31.cloned.1.call-start = ((), (), s32[]{:S(2)}) async-start(), calls=%async_computation.33 | async-start | bytes 2621440 | tf_op jit(solution)/shard_map/all_gather | solution.py:248
  2048.9 107.4 %all-gather.35.cloned.1.call-start = ((), (), s32[]{:S(2)}) async-start(), calls=%async_computation.35 | async-start | bytes 5242880 | tf_op jit(solution)/shard_map/all_gather | solution.py:250
  2056.7 136.0 %all-gather.37.cloned.1.call-start = ((), (), s32[]{:S(2)}) async-start(), calls=%async_computation.36 | async-start | bytes 5242880 | tf_op jit(solution)/shard_map/all_gather | solution.py:251
  2057.3 260.5 %all-reduce.6.cloned.1.call-start = ((), (), s32[]{:S(2)}) async-start(), calls=%async_computation.39 | async-start | bytes 131072 | tf_op jit(solution)/shard_map/psum | solution.py:341
  2057.7 9.6 copy-start.17
  2074.1 9.9 copy-start.8
  2074.1 9.9 copy-start.11
  2092.2 27.4 %copy-start.37 = (bf16[256,128]{1,0:T(8,128)(2,1)S(1)}, bf16[256,128]{1,0:T(8,128)(2,1)}, u32[]{:S(2)}) copy-start(bf16[256,128]{1,0:T(8,128)(2,1)} %param.25) | copy-start | bytes 196612
  2092.8 280.8 %all-reduce.8.cloned.1.call-start = ((), (), s32[]{:S(2)}) async-start(), calls=%async_computation.40 | async-start | bytes 3080192 | tf_op jit(solution)/shard_map/psum | solution.py:47
  2099.7 22.8 copy-start.23
  2099.7 22.8 copy-start.39
  2161.7 36.6 %copy-start.32 = (bf16[256,256]{1,0:T(8,128)(2,1)S(1)}, bf16[256,256]{1,0:T(8,128)(2,1)}, u32[]{:S(2)}) copy-start(bf16[256,256]{1,0:T(8,128)(2,1)} %param.27) | copy-start | bytes 393220
  2198.2 6.2 copy-start.34
  2198.2 322.3 %reduce-scatter.38.cloned.1.call-start = ((), (), s32[]{:S(2)}) async-start(), calls=%async_computation.38 | async-start | bytes 10485760 | tf_op jit(solution)/shard_map/reduce_scatter | solution.py:41
  2198.2 6.1 copy-start.7
  2211.4 457.6 %reduce-scatter.30.cloned.1.call-start = ((), (), s32[]{:S(2)}) async-start(), calls=%async_computation.25 | async-start | bytes 10485760 | tf_op jit(solution)/shard_map/reduce_scatter | solution.py:41
  2228.9 291.6 %copy-start.18 = (bf16[2048,256]{1,0:T(8,128)(2,1)S(1)}, bf16[2048,256]{1,0:T(8,128)(2,1)}, u32[]{:S(2)}) copy-start(bf16[2048,256]{1,0:T(8,128)(2,1)} %param.21) | copy-start | bytes 3145732
  2228.9 291.6 %copy-start.47 = (f32[2048]{0:T(1024)S(1)}, f32[2048]{0:T(1024)}, u32[]{:S(2)}) copy-start(f32[2048]{0:T(1024)} %copy-done.46) | copy-start | bytes 24580
  2228.9 291.6 %copy-start.59 = (f32[256]{0:T(256)S(1)}, f32[256]{0:T(256)}, u32[]{:S(2)}) copy-start(f32[256]{0:T(256)} %copy-done.58) | copy-start | bytes 3076
  2228.9 294.3 %copy-start.56 = (f32[1024]{0:T(1024)S(1)}, f32[1024]{0:T(1024)}, u32[]{:S(2)}) copy-start(f32[1024]{0:T(1024)} %copy-done.55) | copy-start | bytes 12292
  2228.9 294.3 %copy-start.62 = (f32[512]{0:T(512)S(1)}, f32[512]{0:T(512)}, u32[]{:S(2)}) copy-start(f32[512]{0:T(512)} %copy-done.61) | copy-start | bytes 6148
  2228.9 294.3 %copy-start.65 = (f32[256]{0:T(256)S(1)}, f32[256]{0:T(256)}, u32[]{:S(2)}) copy-start(f32[256]{0:T(256)} %get-tuple-element.344) | copy-start | bytes 3076
  2234.2 434.8 %copy-start.3 = (f32[2048,256]{1,0:T(8,128)S(1)}, f32[2048,256]{1,0:T(8,128)}, u32[]{:S(2)}) copy-start(f32[2048,256]{1,0:T(8,128)} %copy-done.2) | copy-start | bytes 6291460
  2234.2 434.8 %copy-start.44 = (f32[2048]{0:T(1024)S(1)}, f32[2048]{0:T(1024)}, u32[]{:S(2)}) copy-start(f32[2048]{0:T(1024)} %copy-done.42) | copy-start | bytes 24580
  2373.6 10.6 copy-start.52
  2577.8 96.0 %copy-start.1 = (bf16[256,704]{0,1:T(8,128)(2,1)S(1)}, bf16[256,704]{0,1:T(8,128)(2,1)}, u32[]{:S(2)}) copy-start(bf16[256,704]{0,1:T(8,128)(2,1)} %param.35) | copy-start | bytes 1081348
  (39 other events, 78.3 us)
Sparse Core Ops, SparseCore 0:
  21.3 81.0 all-gather.14
  106.7 20.1 reduce-scatter.17
  129.4 44.5 reduce-scatter.15
  176.4 44.5 reduce-scatter.19
  223.5 71.3 reduce-scatter.13
  297.3 71.3 reduce-scatter.21
  520.2 34.3 all-gather.16
  561.5 144.6 reduce-scatter.23
  707.7 81.3 all-gather.22
  790.5 79.2 all-gather.18
  872.4 161.4 reduce-scatter.31
  1036.4 162.9 reduce-scatter.25
  1202.0 162.9 reduce-scatter.27
  1375.9 76.1 all-gather.24
  1453.5 76.1 all-gather.26
  1543.4 144.6 reduce-scatter.33
  1700.6 81.1 all-gather.28
  1787.3 43.0 reduce-scatter.35
  1832.0 76.1 all-gather.20
  2047.5 22.5 all-gather.38
  2072.3 22.5 all-gather.32
  2097.0 22.5 all-gather.30
  2121.8 34.4 all-gather.34
  2158.2 34.4 all-gather.36
  2198.3 119.3 all-reduce.5
  2321.4 52.1 all-reduce.7
  2375.8 144.6 reduce-scatter.37
  2522.8 146.1 reduce-scatter.29
